TPU v7x, 256 devices: a whole 4x4x8 slice. The times are simulated.
256 devices in a mesh: segment: 4 (over z_lo, core), zero: 64 (over x, y, z_hi).
Axes of the slice: x: 4, y: 4, z: 8 (z_hi: 4, z_lo: 2; z = z_hi * 2 + z_lo), core: 2. Of those that a mesh axis runs over, the one named last changes fastest.
Arguments:
- inputs: bfloat16 [2, 2, 8192, 2048], P(None, None, 'zero'), may hold values from -6 to 6
- cotangent: bfloat16 [2, 2, 8192, 2048], P(None, None, 'zero'), may hold values from -0.078125 to 0.078125
- norm_gain: bfloat16 [4, 2048], P('segment', 'zero'), may hold values from 0.099609375 to 1.8984375
- proj_in: bfloat16 [4, 2048, 256], P('segment', 'zero'), may hold values from -0.125 to 0.125
- proj_out: bfloat16 [4, 256, 2048], P('segment', 'zero'), may hold values from -0.375 to 0.375
Outputs:
- grad_norm_gain: float32 [4, 2048], P('segment', 'zero')
- grad_proj_in: float32 [4, 2048, 256], P('segment', 'zero')
- grad_proj_out: float32 [4, 256, 2048], P('segment', 'zero')
All inputs are finite; a program needn't handle non-finite values.
Results may differ from a plain program's by a relative error of at most 0.012.
Values may be sent and summed in bfloat16 or wider, within the bound.
No kernel may reach another device: no remote copies, remote signals or barrier semaphores. Data moves between devices by JAX's collectives and lax.ppermute only.
A program may use at most 64 MiB of HBM per device.

v0:
```python
import jax
import jax.numpy as jnp
from jax import lax
from jax.sharding import PartitionSpec as P

gelu_coeff = 0.7978845608028654
cubic_coeff = 0.044715
norm_eps = 1e-05


def partner(value, axis, stride):
    return lax.ppermute(value, axis, [(i, i ^ 1 << stride) for i in range(lax.axis_size(axis))])


def from_behind(block, axis, distance):
    devices = range(lax.axis_size(axis))
    route = [(i - distance, i) for i in devices if i - distance in devices]
    return lax.ppermute(block, axis, route)


def gelu_tanh(values):
    return (
        0.5
        * values
        * (1.0 + jnp.tanh(gelu_coeff * (values + cubic_coeff * values * values * values)))
    )


def gelu_slope(values):
    inner = jnp.tanh(gelu_coeff * (values + cubic_coeff * values * values * values))
    return 0.5 * (1.0 + inner) + 0.5 * values * (1.0 - inner * inner) * gelu_coeff * (
        1.0 + 3.0 * cubic_coeff * values * values
    )


def contract(left, right, left_dim, right_dim):
    return lax.dot_general(
        left, right, (((left_dim,), (right_dim,)), ((), ())), preferred_element_type=jnp.float32
    )


def layer_forward(state, gain, weight_in, weight_out):
    as_float = state.astype(jnp.float32)
    centered = as_float - jnp.mean(as_float, axis=-1, keepdims=True)
    variance = jnp.mean(centered * centered, axis=-1, keepdims=True)
    recip_std = lax.rsqrt(variance + norm_eps)
    hatted = centered * recip_std
    normed = (hatted * gain.astype(jnp.float32)).astype(jnp.bfloat16)
    preact = jnp.dot(normed, weight_in, preferred_element_type=jnp.float32)
    gelu_out = gelu_tanh(preact).astype(jnp.bfloat16)
    result = (as_float + jnp.dot(gelu_out, weight_out, preferred_element_type=jnp.float32)).astype(
        jnp.bfloat16
    )
    return (result, (hatted, recip_std, normed, preact, gelu_out))


def layer_backward(state, upstream, gain, weight_in, weight_out):
    result, saved = layer_forward(state, gain, weight_in, weight_out)
    hatted, recip_std, normed, preact, gelu_out = saved
    grad_out = contract(gelu_out, upstream, 0, 0)
    grad_act = contract(upstream, weight_out, 1, 1)
    grad_pre = (grad_act * gelu_slope(preact)).astype(jnp.bfloat16)
    grad_in = contract(normed, grad_pre, 0, 0)
    grad_normed = contract(grad_pre, weight_in, 1, 1)
    grad_gain = jnp.sum(grad_normed * hatted, axis=0)
    grad_hat = grad_normed * gain.astype(jnp.float32)
    through = recip_std * (
        grad_hat
        - jnp.mean(grad_hat, axis=-1, keepdims=True)
        - hatted * jnp.mean(grad_hat * hatted, axis=-1, keepdims=True)
    )
    grad_state = (upstream.astype(jnp.float32) + through).astype(jnp.bfloat16)
    return (grad_state, grad_in, grad_out, grad_gain)


def pick_slot(stack, index):
    return lax.dynamic_index_in_dim(stack, index, 0, keepdims=False)


def keep_slot(stack, index, valid, value):
    merged = jnp.where(valid, value, pick_slot(stack, index))
    return lax.dynamic_update_index_in_dim(stack, merged, index, 0)


def per_device(inputs, cotangent, norm_gain, proj_in, proj_out):
    segment_count = lax.axis_size("segment")
    segment_idx = lax.axis_index("segment")
    bit_count = segment_count.bit_length() - 1
    mirror_in, mirror_out, mirror_gain = (proj_in, proj_out, norm_gain)
    for bit_pos in range(bit_count):
        mirror_in, mirror_out, mirror_gain = partner(
            (mirror_in, mirror_out, mirror_gain), "segment", bit_pos
        )
    gathered = (
        lax.all_gather(proj_in, "zero", axis=1, tiled=True),
        lax.all_gather(mirror_in, "zero", axis=1, tiled=True),
        lax.all_gather(proj_out, "zero", axis=1, tiled=True),
        lax.all_gather(mirror_out, "zero", axis=1, tiled=True),
        lax.all_gather(norm_gain, "zero", axis=1, tiled=True),
        lax.all_gather(mirror_gain, "zero", axis=1, tiled=True),
    )
    down_in, upper_in = (gathered[0][0], gathered[1][0])
    down_out, upper_out = (gathered[2][0], gathered[3][0])
    down_gain, upper_gain = (gathered[4][0], gathered[5][0])
    micro_count = inputs.shape[1]
    rows = inputs.shape[2]
    width = inputs.shape[3]
    tick_total = micro_count + segment_count - 1
    is_first = segment_idx == 0
    is_last = segment_idx == segment_count - 1
    last_slot = micro_count - 1
    stash_down = jnp.zeros((micro_count, rows, width), jnp.bfloat16)
    stash_upper = jnp.zeros((micro_count, rows, width), jnp.bfloat16)
    recv_down = jnp.zeros((rows, width), jnp.bfloat16)
    recv_upper = jnp.zeros((rows, width), jnp.bfloat16)
    for tick_num in range(tick_total):
        micro_down = tick_num - segment_idx
        micro_upper = tick_num - (segment_count - 1 - segment_idx)
        valid_down = (micro_down >= 0) & (micro_down < micro_count)
        valid_upper = (micro_upper >= 0) & (micro_upper < micro_count)
        slot_down = jnp.clip(micro_down, 0, last_slot)
        slot_upper = jnp.clip(micro_upper, 0, last_slot)
        enter_down = jnp.where(is_first, pick_slot(inputs[0], slot_down), recv_down)
        enter_upper = jnp.where(is_last, pick_slot(inputs[1], slot_upper), recv_upper)
        stash_down = keep_slot(stash_down, slot_down, valid_down, enter_down)
        stash_upper = keep_slot(stash_upper, slot_upper, valid_upper, enter_upper)
        leave_down, unused_down = layer_forward(enter_down, down_gain, down_in, down_out)
        leave_upper, unused_upper = layer_forward(enter_upper, upper_gain, upper_in, upper_out)
        if tick_num + 1 < tick_total:
            recv_down = from_behind(leave_down, "segment", 1)
            recv_upper = from_behind(leave_upper, "segment", -1)
    acc_down_in = jnp.zeros(down_in.shape, jnp.float32)
    acc_down_out = jnp.zeros(down_out.shape, jnp.float32)
    acc_down_gain = jnp.zeros(down_gain.shape, jnp.float32)
    acc_upper_in = jnp.zeros(upper_in.shape, jnp.float32)
    acc_upper_out = jnp.zeros(upper_out.shape, jnp.float32)
    acc_upper_gain = jnp.zeros(upper_gain.shape, jnp.float32)
    back_recv_down = jnp.zeros((rows, width), jnp.bfloat16)
    back_recv_upper = jnp.zeros((rows, width), jnp.bfloat16)
    for tick_num in range(tick_total):
        micro_down = tick_num - (segment_count - 1 - segment_idx)
        micro_upper = tick_num - segment_idx
        valid_down = (micro_down >= 0) & (micro_down < micro_count)
        valid_upper = (micro_upper >= 0) & (micro_upper < micro_count)
        slot_down = jnp.clip(micro_down, 0, last_slot)
        slot_upper = jnp.clip(micro_upper, 0, last_slot)
        upstream_down = jnp.where(is_last, pick_slot(cotangent[0], slot_down), back_recv_down)
        upstream_upper = jnp.where(is_first, pick_slot(cotangent[1], slot_upper), back_recv_upper)
        back_down, grad_in, grad_out, grad_gain = layer_backward(
            pick_slot(stash_down, slot_down), upstream_down, down_gain, down_in, down_out
        )
        acc_down_in = acc_down_in + jnp.where(valid_down, grad_in, 0.0)
        acc_down_out = acc_down_out + jnp.where(valid_down, grad_out, 0.0)
        acc_down_gain = acc_down_gain + jnp.where(valid_down, grad_gain, 0.0)
        back_upper, grad_in, grad_out, grad_gain = layer_backward(
            pick_slot(stash_upper, slot_upper), upstream_upper, upper_gain, upper_in, upper_out
        )
        acc_upper_in = acc_upper_in + jnp.where(valid_upper, grad_in, 0.0)
        acc_upper_out = acc_upper_out + jnp.where(valid_upper, grad_out, 0.0)
        acc_upper_gain = acc_upper_gain + jnp.where(valid_upper, grad_gain, 0.0)
        if tick_num + 1 < tick_total:
            back_recv_down = from_behind(back_down, "segment", -1)
            back_recv_upper = from_behind(back_upper, "segment", 1)
    passed_in, passed_out, passed_gain = (acc_upper_in, acc_upper_out, acc_upper_gain)
    for bit_pos in range(bit_count):
        passed_in, passed_out, passed_gain = (
            partner(passed_in.astype(jnp.bfloat16), "segment", bit_pos).astype(passed_in.dtype),
            partner(passed_out.astype(jnp.bfloat16), "segment", bit_pos).astype(passed_out.dtype),
            partner(passed_gain.astype(jnp.bfloat16), "segment", bit_pos).astype(passed_gain.dtype),
        )
    total_in, total_out, total_gain = (
        lax.psum_scatter(acc_down_in + passed_in, "zero", scatter_dimension=0, tiled=True),
        lax.psum_scatter(acc_down_out + passed_out, "zero", scatter_dimension=0, tiled=True),
        lax.psum_scatter(acc_down_gain + passed_gain, "zero", scatter_dimension=0, tiled=True),
    )
    return (total_gain[None], total_in[None], total_out[None])


def solution(mesh):
    return jax.shard_map(
        per_device,
        mesh=mesh,
        in_specs=(
            P(None, None, "zero", None),
            P(None, None, "zero", None),
            P("segment", "zero"),
            P("segment", "zero", None),
            P("segment", "zero", None),
        ),
        out_specs=(P("segment", "zero"), P("segment", "zero", None), P("segment", "zero", None)),
        check_vma=False,
    )
```

profile of v0, /device:TPU:32, one launch (start us, length us, event | category | flops | bytes accessed | tf_op | source)
XLA Modules:
  0.0 1634.1 jit_solution(740983835067146527)
XLA Ops:
  7.2 1.4 copy.10
  9.5 1.4 collective-permute-done.8
  10.9 1.8 collective-permute-start.9
  12.7 2.1 collective-permute-done.9
  16.1 1.7 fusion.806
  18.5 1.9 collective-permute-start.13
  20.5 1.9 collective-permute-done.13
  27.2 1.6 fusion.807
  28.8 1.8 collective-permute-start.11
  30.8 1.5 collective-permute-done.11
  32.5 199.0 %all-reduce.4 = (bf16[2048]{0:T(1024)(128)(2,1)S(1)}, bf16[2048]{0:T(1024)(128)(2,1)S(1)}) all-reduce(bf16[2048]{0:T(1024)(128)(2,1)S(1)} %dynamic-update-slice.1, bf16[2048]{0:T(1024)(128)(2,1)S(1)} %dynamic-update-slice), channel_id=1, replica_groups=mesh['segment'=4,'zero'=64] {'zero'}, use_global_device_ids=true, to_apply=%add.1 | all-reduce | flops 4096 | bytes 16384
  231.6 3.2 copy.12
  234.8 3.5 fusion.18
  238.3 1.9 collective-permute-start
  241.1 8.1 all-gather.9.cloned.1.call-done
  249.2 3.2 copy.13
  252.4 75.1 %all-gather.11.cloned.1.call-done = bf16[1,2048,256]{2,1,0:T(8,128)(2,1)} async-done(((bf16[1,32,256]{2,1,0:T(8,128)(2,1)}), bf16[1,2048,256]{2,1,0:T(8,128)(2,1)}) %all-gather.11.cloned.1.call-update) | async-done | bytes 1048592 | tf_op jit(solution)/shard_map/all_gather | solution.py:96
  327.5 3.2 fusion.22
  330.7 1.9 collective-permute-start.14
  332.6 1.4 convert_reduce_fusion.16
  335.2 3.5 fusion.19
  338.6 3.2 collective-permute-start.1
  346.3 3.5 fusion.23
  349.8 2.8 collective-permute-start.15
  352.6 1.3 bitcast_dynamic-update-slice_fusion.3
  354.8 1.3 convert_reduce_fusion.15
  357.2 3.5 fusion.20
  360.7 2.6 collective-permute-start.2
  363.3 1.3 bitcast_dynamic-update-slice_fusion.7
  367.9 3.5 fusion.24
  371.3 3.1 collective-permute-start.16
  374.4 1.3 bitcast_dynamic-update-slice_fusion.2
  379.0 3.5 fusion.21
  382.5 2.0 collective-permute-start.3
  384.5 1.3 bitcast_dynamic-update-slice_fusion.6
  389.1 3.5 fusion.25
  392.6 3.5 collective-permute-start.17
  397.4 1.3 bitcast_dynamic-update-slice_fusion.5
  401.1 1.6 fusion.87
  403.3 2.3 collective-permute-start.4
  410.9 1.6 fusion.171
  413.1 2.3 collective-permute-start.18
  419.8 3.3 collective-permute-start.5
  425.9 2.3 collective-permute-start.19
  432.1 3.8 collective-permute-start.6
  438.7 1.9 collective-permute-start.20
  441.2 1.3 collective-permute-done.6
  443.1 6.1 collective-permute-done.20
  451.5 1.9 collective-permute-start.21
  455.1 6.9 collective-permute-done.21
  463.8 1.9 collective-permute-start.7
  468.8 8.8 collective-permute-done.7
  478.4 16.5 %collective-permute-done.27 = bf16[256,2048]{1,0:T(8,128)(2,1)S(1)} collective-permute-done((bf16[256,2048]{1,0:T(8,128)(2,1)S(1)}, bf16[256,2048]{1,0:T(8,128)(2,1)S(1)}, u32[]{:S(2)}, u32[]{:S(2)}) %collective-permute-start.27) | collective-permute-done | bytes 1048608 | tf_op jit(solution)/shard_map/ppermute | solution.py:12
  494.9 2.0 convert_add_fusion
  497.5 1.4 convolution_select_fusion.19
  498.9 2.6 collective-permute-start.25
  505.6 17.5 %collective-permute-done.25 = bf16[2048,256]{1,0:T(8,128)(2,1)S(1)} collective-permute-done((bf16[2048,256]{1,0:T(8,128)(2,1)}, bf16[2048,256]{1,0:T(8,128)(2,1)S(1)}, u32[]{:S(2)}, u32[]{:S(2)}) %collective-permute-start.25) | collective-permute-done | bytes 1048608 | tf_op jit(solution)/shard_map/ppermute | solution.py:12
  523.1 1.9 convert_add_fusion.1
  525.8 1.8 fusion.41
  529.9 2.7 collective-permute-done.23
  532.7 194.3 %all-reduce.2 = f32[2048]{0:T(1024)S(1)} all-reduce(f32[2048]{0:T(1024)S(1)} %convert_add_fusion.2), channel_id=2, replica_groups=mesh['segment'=4,'zero'=64] {'zero'}, use_global_device_ids=true, to_apply=%region_62.63.clone | all-reduce | flops 2048 | bytes 16384
  727.7 509.5 %all-reduce.7.cloned.1.call-done = f32[256,2048]{1,0:T(8,128)} async-done(((f32[256,2048]{1,0:T(8,128)}), f32[256,2048]{1,0:T(8,128)}) %all-reduce.7.cloned.1.call-update) | async-done | bytes 2097168
  1237.1 1.5 dynamic-slice_bitcast_fusion
  1238.6 388.4 %reduce-scatter.2.cloned.1.call-done = f32[32,256]{1,0:T(8,128)} async-done(((f32[2048,256]{1,0:T(8,128)}), f32[32,256]{1,0:T(8,128)}) %reduce-scatter.2.cloned.1.call-update) | async-done | bytes 32784 | tf_op jit(solution)/shard_map/reduce_scatter | solution.py:172
  (305 shorter events, 66.3 us)
Async XLA Ops:
  7.2 224.5 %all-gather.5.cloned.1.call-start = ((), (), s32[]{:S(2)}) async-start(), calls=%async_computation.1 | async-start | bytes 2129920 | tf_op jit(solution)/shard_map/all_gather | solution.py:97
  8.6 226.2 %all-gather.7.cloned.1.call-start = ((), (), s32[]{:S(2)}) async-start(), calls=%async_computation.2 | async-start | bytes 1064960 | tf_op jit(solution)/shard_map/all_gather | solution.py:95
  9.3 239.9 %all-gather.9.cloned.1.call-start = ((), (), s32[]{:S(2)}) async-start(), calls=%async_computation.3 | async-start | bytes 2129920 | tf_op jit(solution)/shard_map/all_gather | solution.py:98
  9.4 1.5 collective-permute-start.8
  10.9 3.9 collective-permute-start.9
  15.5 312.0 %all-gather.11.cloned.1.call-start = ((), (), s32[]{:S(2)}) async-start(), calls=%async_computation.4 | async-start | bytes 1064960 | tf_op jit(solution)/shard_map/all_gather | solution.py:96
  15.5 3.0 collective-permute-start.12
  15.6 13.2 collective-permute-start.10
  17.8 7.1 copy-start
  17.8 5.5 copy-start.47
  18.5 3.8 collective-permute-start.13
  23.0 1214.2 %all-reduce.7.cloned.1.call-start = ((), (), s32[]{:S(2)}) async-start(), calls=%async_computation.6 | async-start | bytes 4194304
  27.2 3.4 copy-start.57
  28.8 3.6 collective-permute-start.11
  238.3 94.3 %collective-permute-start = (bf16[128,2048]{1,0:T(8,128)(2,1)}, bf16[128,2048]{1,0:T(8,128)(2,1)}, u32[]{:S(2)}, u32[]{:S(2)}) collective-permute-start(bf16[128,2048]{1,0:T(8,128)(2,1)} %fusion.18), channel_id=1, source_target_pairs={{0,64},{64,128},{128,192},{1,65},{65,129},{129,193},{2,66},{66,130... | collective-permute-start | bytes 1572872 | tf_op jit(solution)/shard_map/ppermute | solution.py:18
  330.7 13.2 collective-permute-start.14
  338.6 16.1 collective-permute-start.1
  349.7 5.0 copy-start.1
  349.8 15.7 collective-permute-start.15
  360.7 16.0 collective-permute-start.2
  371.3 5.3 copy-start.2
  371.3 15.4 collective-permute-start.16
  382.5 14.8 collective-permute-start.3
  392.6 4.8 copy-start.3
  392.6 4.8 copy-start.14
  392.6 15.0 collective-permute-start.17
  399.2 3.5 copy-start.31
  399.2 20.0 %copy-start.33 = (f32[128]{0:T(128)}, f32[128]{0:T(128)S(1)}, u32[]{:S(2)}) copy-start(f32[128]{0:T(128)S(1)} %get-tuple-element.77) | copy-start | bytes 1540
  399.5 3.2 copy-start.46
  399.5 31.9 %copy-start.37 = (f32[128]{0:T(128)}, f32[128]{0:T(128)S(1)}, u32[]{:S(2)}) copy-start(f32[128]{0:T(128)S(1)} %broadcast_multiply_fusion.23) | copy-start | bytes 1540
  399.5 63.6 %copy-start.35 = (f32[128]{0:T(128)}, f32[128]{0:T(128)S(1)}, u32[]{:S(2)}) copy-start(f32[128]{0:T(128)S(1)} %broadcast_multiply_fusion.20) | copy-start | bytes 1540
  399.9 6.8 copy-start.50
  403.3 14.2 collective-permute-start.4
  405.6 13.6 copy-start.43
  405.6 25.9 %copy-start.41 = (f32[128]{0:T(128)}, f32[128]{0:T(128)S(1)}, u32[]{:S(2)}) copy-start(f32[128]{0:T(128)S(1)} %add_rsqrt_fusion.11) | copy-start | bytes 1540
  405.6 57.6 %copy-start.39 = (f32[128]{0:T(128)}, f32[128]{0:T(128)S(1)}, u32[]{:S(2)}) copy-start(f32[128]{0:T(128)S(1)} %add_rsqrt_fusion.10) | copy-start | bytes 1540
  410.9 56.5 %copy-start.44 = (f32[128]{0:T(128)}, f32[128]{0:T(128)S(1)}, u32[]{:S(2)}) copy-start(f32[128]{0:T(128)S(1)} %get-tuple-element.73) | copy-start | bytes 1540
  413.1 10.5 collective-permute-start.18
  415.4 52.0 %copy-start.48 = (f32[128]{0:T(128)}, f32[128]{0:T(128)S(1)}, u32[]{:S(2)}) copy-start(f32[128]{0:T(128)S(1)} %add_rsqrt_fusion) | copy-start | bytes 1540
  419.8 10.0 collective-permute-start.5
  425.9 10.5 collective-permute-start.19
  432.1 10.5 collective-permute-start.6
  438.7 10.5 collective-permute-start.20
  451.5 10.5 collective-permute-start.21
  463.1 3.1 collective-permute-start.26
  463.8 13.8 collective-permute-start.7
  466.2 28.7 %collective-permute-start.27 = (bf16[256,2048]{1,0:T(8,128)(2,1)S(1)}, bf16[256,2048]{1,0:T(8,128)(2,1)S(1)}, u32[]{:S(2)}, u32[]{:S(2)}) collective-permute-start(bf16[256,2048]{1,0:T(8,128)(2,1)S(1)} %collective-permute-done.26), channel_id=1, source_target_pairs={{0,128},{64,192},{128,0},{192,64},{1,129},{65,193},{129,1},{193,65... | collective-permute-start | bytes 3145736 | tf_op jit(solution)/shard_map/ppermute | solution.py:12
  468.0 30.9 %collective-permute-start.24 = (bf16[2048,256]{1,0:T(8,128)(2,1)S(1)}, bf16[2048,256]{1,0:T(8,128)(2,1)}, u32[]{:S(2)}, u32[]{:S(2)}) collective-permute-start(bf16[2048,256]{1,0:T(8,128)(2,1)S(1)} %fusion.17), channel_id=1, source_target_pairs={{0,64},{64,0},{128,192},{192,128},{1,65},{65,1},{129,193},{193,129... | collective-permute-start | bytes 3145736 | tf_op jit(solution)/shard_map/ppermute | solution.py:12
  496.9 4.6 copy-start.34
  496.9 1130.1 %reduce-scatter.2.cloned.1.call-start = ((), (), s32[]{:S(2)}) async-start(), calls=%async_computation.5 | async-start | bytes 2129920 | tf_op jit(solution)/shard_map/reduce_scatter | solution.py:172
  498.9 3.8 copy-start.38
  498.9 3.8 copy-start.42
  498.9 24.2 %collective-permute-start.25 = (bf16[2048,256]{1,0:T(8,128)(2,1)}, bf16[2048,256]{1,0:T(8,128)(2,1)S(1)}, u32[]{:S(2)}, u32[]{:S(2)}) collective-permute-start(bf16[2048,256]{1,0:T(8,128)(2,1)} %collective-permute-done.24), channel_id=1, source_target_pairs={{0,128},{64,192},{128,0},{192,64},{1,129},{65,193},{129,1},{193,65... | collective-permute-start | bytes 3145736 | tf_op jit(solution)/shard_map/ppermute | solution.py:12
  505.1 18.0 %copy-start.51 = (f32[128]{0:T(128)S(1)}, f32[128]{0:T(128)}, u32[]{:S(2)}) copy-start(f32[128]{0:T(128)} %copy-done.50) | copy-start | bytes 1540
  505.1 18.0 %copy-start.53 = (f32[128]{0:T(128)S(1)}, f32[128]{0:T(128)}, u32[]{:S(2)}) copy-start(f32[128]{0:T(128)} %copy-done.52) | copy-start | bytes 1540
  525.1 2.5 copy-start.29
  525.1 2.5 copy-start.30
  525.1 4.4 copy-start.55
  525.7 6.9 copy-start.23
  525.7 6.9 copy-start.24
  525.7 6.9 copy-start.25
  525.7 6.9 copy-start.26
  527.6 1.4 collective-permute-start.22
  529.0 3.7 collective-permute-start.23
  (28 other events, 33.9 us)
Sparse Core Ops, SparseCore 0:
  11.9 80.6 all-gather.4
  95.9 73.5 all-gather.6
  173.4 75.8 all-gather.8
  252.4 75.0 all-gather.10
  497.0 740.0 all-reduce.6
  1240.1 386.9 reduce-scatter.1
where the time goes:
time: 1640 us; the launch traced here: 1630 us
  waiting for transfers between devices  1050 us (64%)
  blocking collectives  393 us (24%)
  matrix products  63.4 us (4%)
  starting transfers between devices  51.3 us (3%)
  local copies, waits for them, and re-layouts  30.6 us (2%)
  other arithmetic  27.9 us (2%)
  between operations  17.7 us (1%)
    unnamed x7, waiting for transfers between devices  510 us
    unnamed x2, blocking collectives  393 us
    reduce_scatter x1, waiting for transfers between devices, per_device(): lax.psum_scatter(acc_down_in + passed_in, 'zero', scatter_dimension=0, ti...  388 us
    all_gather x1, waiting for transfers between devices, per_device(): lax.all_gather(mirror_in, 'zero', axis=1, tiled=True)  75.1 us
    ppermute x12, waiting for transfers between devices, partner(): lax.ppermute(value, axis, [(i, i ^ 1 << stride) for i in range(lax.axis_s...  43.7 us
    ppermute x16, starting transfers between devices, from_behind(): return lax.ppermute(block, axis, route)  40.8 us
  transfers between devices with their start and end apart: 34, of which 17 were waited for; matrix products, arithmetic and copies ran while one was open for 7% of the time, Pallas kernels for 0%

commit v1 on v0

--- a/solution.py
+++ b/solution.py
@@ -6,6 +6,19 @@
 gelu_coeff = 0.7978845608028654
 cubic_coeff = 0.044715
 norm_eps = 1e-05
+
+
+def apply_sources_all_for(buf):
+    answer = jnp.concatenate(
+        lax.all_to_all(
+            jnp.stack([buf for _ in range(lax.psum(1, axis_name="zero"))]),
+            split_axis=0,
+            axis_name="zero",
+            concat_axis=0,
+        ),
+        1,
+    )
+    return answer
 
 
 def partner(value, axis, stride):
@@ -93,7 +106,7 @@
         )
     gathered = (
         lax.all_gather(proj_in, "zero", axis=1, tiled=True),
-        lax.all_gather(mirror_in, "zero", axis=1, tiled=True),
+        apply_sources_all_for(mirror_in),
         lax.all_gather(proj_out, "zero", axis=1, tiled=True),
         lax.all_gather(mirror_out, "zero", axis=1, tiled=True),
         lax.all_gather(norm_gain, "zero", axis=1, tiled=True),

time: 1640 us -> 1590 us (0.970)
  waiting for transfers between devices: 1050 us -> 976 us
    all_gather x1 -> x0, waiting for transfers between devices: 75.1 us -> none  [per_device(): lax.all_gather(mirror_in, 'zero', axis=1, tiled=True)]
    unnamed x7 -> x6, waiting for transfers between devices: 510 us -> 508 us
  transfers between devices with their start and end apart: 34 -> 34, of which waited for: 17 -> 11; matrix products, arithmetic and copies ran while one was open for 7% -> 7% of each run, Pallas kernels for 0% -> 0%
where the time goes in v1:
time: 1590 us; the launch traced here: 1580 us
  waiting for transfers between devices  976 us (61%)
  blocking collectives  388 us (24%)
  matrix products  74.8 us (5%)
  starting transfers between devices  63.5 us (4%)
  local copies, waits for them, and re-layouts  31.3 us (2%)
  other arithmetic  26.9 us (2%)
  between operations  17.4 us (1%)
    unnamed x6, waiting for transfers between devices  508 us
    reduce_scatter x1, waiting for transfers between devices, per_device(): lax.psum_scatter(acc_down_in + passed_in, 'zero', scatter_dimension=0, ti...  388 us
    unnamed x2, blocking collectives  388 us
    ppermute x12, waiting for transfers between devices, partner(): lax.ppermute(value, axis, [(i, i ^ 1 << stride) for i in range(lax.axis_s...  55.6 us
    ppermute x16, starting transfers between devices, from_behind(): return lax.ppermute(block, axis, route)  42.3 us
    dot_general x40, matrix products, contract(): lax.dot_general(left, right, (((left_dim,), (right_dim,)), ((), ())), pre...  37.5 us
  transfers between devices with their start and end apart: 34, of which 11 were waited for; matrix products, arithmetic and copies ran while one was open for 7% of the time, Pallas kernels for 0%

profile of v1, /device:TPU:32, one launch (start us, length us, event | category | flops | bytes accessed | tf_op | source)
XLA Modules:
  0.0 1577.7 jit_solution(17640158877081594445)
XLA Ops:
  7.2 1.4 copy.10
  10.0 1.8 fusion.772
  12.5 1.9 collective-permute-start.9
  14.7 3.5 collective-permute-done.13
  19.3 13.1 all-to-all-start
  37.1 1.6 fusion.773
  39.9 14.2 collective-permute-done.11
  54.3 199.1 %all-reduce.4 = (bf16[2048]{0:T(1024)(128)(2,1)S(1)}, bf16[2048]{0:T(1024)(128)(2,1)S(1)}) all-reduce(bf16[2048]{0:T(1024)(128)(2,1)S(1)} %dynamic-update-slice.1, bf16[2048]{0:T(1024)(128)(2,1)S(1)} %dynamic-update-slice), channel_id=1, replica_groups=mesh['segment'=4,'zero'=64] {'zero'}, use_global_device_ids=true, to_apply=%add.1 | all-reduce | flops 4096 | bytes 16384
  253.5 3.2 copy.12
  256.7 3.5 fusion.18
  260.2 1.9 collective-permute-start
  263.0 3.2 copy.13
  266.2 3.2 fusion.22
  269.3 3.6 collective-permute-start.14
  273.0 1.4 convert_reduce_fusion.16
  275.6 3.5 fusion.19
  279.1 2.1 collective-permute-start.1
  285.6 3.5 fusion.23
  289.1 3.9 collective-permute-start.15
  293.1 1.3 bitcast_dynamic-update-slice_fusion.3
  297.7 3.5 fusion.20
  301.2 1.9 collective-permute-start.2
  303.1 1.3 bitcast_dynamic-update-slice_fusion.7
  307.7 3.5 fusion.24
  311.2 3.8 collective-permute-start.16
  314.9 1.3 bitcast_dynamic-update-slice_fusion.2
  319.5 3.5 fusion.21
  323.0 1.9 collective-permute-start.3
  325.0 1.3 bitcast_dynamic-update-slice_fusion.6
  329.6 3.5 fusion.25
  333.1 3.6 collective-permute-start.17
  341.6 1.6 fusion.87
  343.8 2.3 collective-permute-start.4
  349.2 1.6 fusion.305
  351.9 3.0 fusion.171
  355.6 2.3 collective-permute-start.18
  357.9 1.6 fusion.301
  359.5 1.6 fusion.297
  361.1 1.6 fusion.293
  362.7 1.6 fusion.289
  367.1 3.3 collective-permute-start.5
  371.4 2.5 fusion.189
  374.5 2.3 collective-permute-start.19
  380.2 3.6 collective-permute-start.6
  385.6 2.5 fusion.207
  388.6 1.9 collective-permute-start.20
  391.7 7.4 collective-permute-done.20
  399.7 2.5 fusion.225
  402.7 1.9 collective-permute-start.21
  406.3 6.9 collective-permute-done.21
  415.0 1.9 collective-permute-start.7
  420.0 8.8 collective-permute-done.7
  429.6 16.5 %collective-permute-done.27 = bf16[256,2048]{1,0:T(8,128)(2,1)S(1)} collective-permute-done((bf16[256,2048]{1,0:T(8,128)(2,1)S(1)}, bf16[256,2048]{1,0:T(8,128)(2,1)S(1)}, u32[]{:S(2)}, u32[]{:S(2)}) %collective-permute-start.27) | collective-permute-done | bytes 1048608 | tf_op jit(solution)/shard_map/ppermute | solution.py:25
  446.1 2.0 convert_add_fusion
  448.7 1.4 convolution_select_fusion.19
  450.2 2.6 collective-permute-start.25
  456.8 18.5 %collective-permute-done.25 = bf16[2048,256]{1,0:T(8,128)(2,1)S(1)} collective-permute-done((bf16[2048,256]{1,0:T(8,128)(2,1)}, bf16[2048,256]{1,0:T(8,128)(2,1)S(1)}, u32[]{:S(2)}, u32[]{:S(2)}) %collective-permute-start.25) | collective-permute-done | bytes 1048608 | tf_op jit(solution)/shard_map/ppermute | solution.py:25
  475.3 1.9 convert_add_fusion.1
  477.9 1.8 fusion.41
  482.0 2.8 collective-permute-done.23
  484.9 188.7 %all-reduce.2 = f32[2048]{0:T(1024)S(1)} all-reduce(f32[2048]{0:T(1024)S(1)} %convert_add_fusion.2), channel_id=2, replica_groups=mesh['segment'=4,'zero'=64] {'zero'}, use_global_device_ids=true, to_apply=%region_62.63.clone | all-reduce | flops 2048 | bytes 16384
  674.2 507.2 %all-reduce.7.cloned.1.call-done = f32[256,2048]{1,0:T(8,128)} async-done(((f32[256,2048]{1,0:T(8,128)}), f32[256,2048]{1,0:T(8,128)}) %all-reduce.7.cloned.1.call-update) | async-done | bytes 2097168
  1181.4 1.5 dynamic-slice_bitcast_fusion
  1182.9 388.1 %reduce-scatter.2.cloned.1.call-done = f32[32,256]{1,0:T(8,128)} async-done(((f32[2048,256]{1,0:T(8,128)}), f32[32,256]{1,0:T(8,128)}) %reduce-scatter.2.cloned.1.call-update) | async-done | bytes 32784 | tf_op jit(solution)/shard_map/reduce_scatter | solution.py:185
  (303 shorter events, 64.4 us)
Async XLA Ops:
  7.2 246.3 %all-gather.4.cloned.1.call-start = ((), (), s32[]{:S(2)}) async-start(), calls=%async_computation.2 | async-start | bytes 2129920 | tf_op jit(solution)/shard_map/all_gather | solution.py:110
  8.6 248.1 %all-gather.6.cloned.1.call-start = ((), (), s32[]{:S(2)}) async-start(), calls=%async_computation.3 | async-start | bytes 1064960 | tf_op jit(solution)/shard_map/all_gather | solution.py:108
  9.3 3.2 collective-permute-start.8
  9.4 5.0 collective-permute-start.12
  9.9 28.7 %collective-permute-start.10 = (bf16[1,32]{1,0:T(2,128)(2,1)}, bf16[1,32]{1,0:T(2,128)(2,1)S(1)}, u32[]{:S(2)}, u32[]{:S(2)}) collective-permute-start(bf16[1,32]{1,0:T(2,128)(2,1)} %param.7), channel_id=1, source_target_pairs={{0,64},{64,0},{128,192},{192,128},{1,65},{65,1},{129,193},{193,129... | collective-permute-start | bytes 200 | tf_op jit(solution)/shard_map/ppermute | solution.py:25
  11.8 21.4 %copy-start = (bf16[1,2,128,2048]{3,2,1,0:T(8,128)(2,1)}, bf16[1,2,128,2048]{3,2,1,0:T(8,128)(2,1)S(1)}, u32[]{:S(2)}) copy-start(bf16[1,2,128,2048]{3,2,1,0:T(8,128)(2,1)S(1)} %get-tuple-element.59) | copy-start | bytes 3145732
  12.3 21.2 %copy-start.47 = (u32[256]{0:T(256)S(1)}, u32[256]{0:T(256)}, u32[]{:S(2)}) copy-start(u32[256]{0:T(256)} %constant.226) | copy-start | bytes 3076
  12.5 19.9 %collective-permute-start.9 = (bf16[1,4,2048]{2,0,1:T(2,128)(2,1)S(1)}, bf16[1,4,2048]{2,0,1:T(2,128)(2,1)S(1)}, u32[]{:S(2)}, u32[]{:S(2)}) collective-permute-start(bf16[1,4,2048]{2,0,1:T(2,128)(2,1)S(1)} %collective-permute-done.8), channel_id=1, source_target_pairs={{0,128},{64,192},{128,0},{192,64},{1,129},{65,193},{129,1},{193,65... | collective-permute-start | bytes 49160 | tf_op jit(solution)/shard_map/ppermute | solution.py:25
  14.4 3.7 collective-permute-start.13
  19.3 246.9 %all-to-all-start = ((bf16[64,1,32,256]{3,2,1,0:T(8,128)(2,1)}), bf16[64,1,32,256]{3,2,1,0:T(8,128)(2,1)}, u32[]{:S(2)}, u32[]{:S(2)}) async-start(bf16[64,1,32,256]{3,2,1,0:T(8,128)(2,1)} %stack.2), calls=%async_computation | async-start | bytes 2097152 | tf_op jit(solution)/shard_map/all_to_all | solution.py:13
  32.4 230.6 %all-gather.8.cloned.1.call-start = ((), (), s32[]{:S(2)}) async-start(), calls=%async_computation.4 | async-start | bytes 2129920 | tf_op jit(solution)/shard_map/all_gather | solution.py:111
  33.2 1148.3 %all-reduce.7.cloned.1.call-start = ((), (), s32[]{:S(2)}) async-start(), calls=%async_computation.6 | async-start | bytes 4194304
  37.1 2.6 copy-start.56
  38.7 15.4 collective-permute-start.11
  260.2 12.8 collective-permute-start
  269.3 13.9 collective-permute-start.14
  279.1 16.2 %collective-permute-start.1 = (bf16[128,2048]{1,0:T(8,128)(2,1)}, bf16[128,2048]{1,0:T(8,128)(2,1)}, u32[]{:S(2)}, u32[]{:S(2)}) collective-permute-start(bf16[128,2048]{1,0:T(8,128)(2,1)} %fusion.19), channel_id=1, source_target_pairs={{0,64},{64,128},{128,192},{1,65},{65,129},{129,193},{2,66},{66,130... | collective-permute-start | bytes 1572872 | tf_op jit(solution)/shard_map/ppermute | solution.py:31
  289.1 6.2 copy-start.2
  289.1 16.2 %collective-permute-start.15 = (bf16[128,2048]{1,0:T(8,128)(2,1)}, bf16[128,2048]{1,0:T(8,128)(2,1)}, u32[]{:S(2)}, u32[]{:S(2)}) collective-permute-start(bf16[128,2048]{1,0:T(8,128)(2,1)} %fusion.23), channel_id=1, source_target_pairs={{64,0},{128,64},{192,128},{65,1},{129,65},{193,129},{66,2},{130,66... | collective-permute-start | bytes 1572872 | tf_op jit(solution)/shard_map/ppermute | solution.py:31
  301.2 16.0 %collective-permute-start.2 = (bf16[128,2048]{1,0:T(8,128)(2,1)}, bf16[128,2048]{1,0:T(8,128)(2,1)}, u32[]{:S(2)}, u32[]{:S(2)}) collective-permute-start(bf16[128,2048]{1,0:T(8,128)(2,1)} %fusion.20), channel_id=1, source_target_pairs={{0,64},{64,128},{128,192},{1,65},{65,129},{129,193},{2,66},{66,130... | collective-permute-start | bytes 1572872 | tf_op jit(solution)/shard_map/ppermute | solution.py:31
  311.2 6.0 copy-start.3
  311.2 16.0 %collective-permute-start.16 = (bf16[128,2048]{1,0:T(8,128)(2,1)}, bf16[128,2048]{1,0:T(8,128)(2,1)}, u32[]{:S(2)}, u32[]{:S(2)}) collective-permute-start(bf16[128,2048]{1,0:T(8,128)(2,1)} %fusion.24), channel_id=1, source_target_pairs={{64,0},{128,64},{192,128},{65,1},{129,65},{193,129},{66,2},{130,66... | collective-permute-start | bytes 1572872 | tf_op jit(solution)/shard_map/ppermute | solution.py:31
  323.0 14.9 collective-permute-start.3
  333.0 4.9 copy-start.4
  333.1 4.9 copy-start.15
  333.1 15.1 collective-permute-start.17
  339.7 3.5 copy-start.31
  339.7 26.8 %copy-start.33 = (f32[128]{0:T(128)}, f32[128]{0:T(128)S(1)}, u32[]{:S(2)}) copy-start(f32[128]{0:T(128)S(1)} %get-tuple-element.77) | copy-start | bytes 1540
  340.0 3.2 copy-start.46
  340.0 39.6 %copy-start.37 = (f32[128]{0:T(128)}, f32[128]{0:T(128)S(1)}, u32[]{:S(2)}) copy-start(f32[128]{0:T(128)S(1)} %broadcast_multiply_fusion.23) | copy-start | bytes 1540
  340.1 74.3 %copy-start.35 = (f32[128]{0:T(128)}, f32[128]{0:T(128)S(1)}, u32[]{:S(2)}) copy-start(f32[128]{0:T(128)S(1)} %broadcast_multiply_fusion.20) | copy-start | bytes 1540
  340.5 6.8 copy-start.50
  343.8 20.9 %collective-permute-start.4 = (bf16[128,2048]{1,0:T(8,128)(2,1)S(1)}, bf16[128,2048]{1,0:T(8,128)(2,1)S(1)}, u32[]{:S(2)}, u32[]{:S(2)}) collective-permute-start(bf16[128,2048]{1,0:T(8,128)(2,1)S(1)} %fusion.92), channel_id=1, source_target_pairs={{64,0},{128,64},{192,128},{65,1},{129,65},{193,129},{66,2},{130,66... | collective-permute-start | bytes 1572872 | tf_op jit(solution)/shard_map/ppermute | solution.py:31
  346.1 20.4 %copy-start.43 = (f32[128]{0:T(128)}, f32[128]{0:T(128)S(1)}, u32[]{:S(2)}) copy-start(f32[128]{0:T(128)S(1)} %add_rsqrt_fusion.12) | copy-start | bytes 1540
  346.1 33.5 %copy-start.41 = (f32[128]{0:T(128)}, f32[128]{0:T(128)S(1)}, u32[]{:S(2)}) copy-start(f32[128]{0:T(128)S(1)} %add_rsqrt_fusion.11) | copy-start | bytes 1540
  346.2 68.2 %copy-start.39 = (f32[128]{0:T(128)}, f32[128]{0:T(128)S(1)}, u32[]{:S(2)}) copy-start(f32[128]{0:T(128)S(1)} %add_rsqrt_fusion.10) | copy-start | bytes 1540
  351.9 66.7 %copy-start.44 = (f32[128]{0:T(128)}, f32[128]{0:T(128)S(1)}, u32[]{:S(2)}) copy-start(f32[128]{0:T(128)S(1)} %get-tuple-element.73) | copy-start | bytes 1540
  355.6 15.3 collective-permute-start.18
  362.7 55.9 %copy-start.48 = (f32[128]{0:T(128)}, f32[128]{0:T(128)S(1)}, u32[]{:S(2)}) copy-start(f32[128]{0:T(128)S(1)} %add_rsqrt_fusion) | copy-start | bytes 1540
  367.1 10.8 collective-permute-start.5
  374.5 10.5 collective-permute-start.19
  380.2 10.9 collective-permute-start.6
  388.6 10.5 collective-permute-start.20
  402.7 10.5 collective-permute-start.21
  414.3 3.1 collective-permute-start.26
  415.0 13.8 collective-permute-start.7
  417.4 28.7 %collective-permute-start.27 = (bf16[256,2048]{1,0:T(8,128)(2,1)S(1)}, bf16[256,2048]{1,0:T(8,128)(2,1)S(1)}, u32[]{:S(2)}, u32[]{:S(2)}) collective-permute-start(bf16[256,2048]{1,0:T(8,128)(2,1)S(1)} %collective-permute-done.26), channel_id=1, source_target_pairs={{0,128},{64,192},{128,0},{192,64},{1,129},{65,193},{129,1},{193,65... | collective-permute-start | bytes 3145736 | tf_op jit(solution)/shard_map/ppermute | solution.py:25
  419.2 30.9 %collective-permute-start.24 = (bf16[2048,256]{1,0:T(8,128)(2,1)S(1)}, bf16[2048,256]{1,0:T(8,128)(2,1)}, u32[]{:S(2)}, u32[]{:S(2)}) collective-permute-start(bf16[2048,256]{1,0:T(8,128)(2,1)S(1)} %fusion.17), channel_id=1, source_target_pairs={{0,64},{64,0},{128,192},{192,128},{1,65},{65,1},{129,193},{193,129... | collective-permute-start | bytes 3145736 | tf_op jit(solution)/shard_map/ppermute | solution.py:25
  448.1 4.6 copy-start.34
  448.1 1122.9 %reduce-scatter.2.cloned.1.call-start = ((), (), s32[]{:S(2)}) async-start(), calls=%async_computation.5 | async-start | bytes 2129920 | tf_op jit(solution)/shard_map/reduce_scatter | solution.py:185
  450.1 3.8 copy-start.38
  450.1 3.8 copy-start.42
  450.2 25.1 %collective-permute-start.25 = (bf16[2048,256]{1,0:T(8,128)(2,1)}, bf16[2048,256]{1,0:T(8,128)(2,1)S(1)}, u32[]{:S(2)}, u32[]{:S(2)}) collective-permute-start(bf16[2048,256]{1,0:T(8,128)(2,1)} %collective-permute-done.24), channel_id=1, source_target_pairs={{0,128},{64,192},{128,0},{192,64},{1,129},{65,193},{129,1},{193,65... | collective-permute-start | bytes 3145736 | tf_op jit(solution)/shard_map/ppermute | solution.py:25
  456.3 19.0 %copy-start.51 = (f32[128]{0:T(128)S(1)}, f32[128]{0:T(128)}, u32[]{:S(2)}) copy-start(f32[128]{0:T(128)} %copy-done.50) | copy-start | bytes 1540
  456.3 19.0 %copy-start.53 = (f32[128]{0:T(128)S(1)}, f32[128]{0:T(128)}, u32[]{:S(2)}) copy-start(f32[128]{0:T(128)} %copy-done.52) | copy-start | bytes 1540
  477.2 2.5 copy-start.29
  477.2 2.5 copy-start.30
  477.3 4.3 copy-start.55
  477.9 6.9 copy-start.23
  477.9 6.9 copy-start.24
  477.9 6.9 copy-start.25
  477.9 7.0 copy-start.26
  479.8 1.4 collective-permute-start.22
  481.2 3.7 collective-permute-start.23
  (27 other events, 34.3 us)
Sparse Core Ops, SparseCore 0:
  11.9 85.4 all-gather.3
  100.7 73.6 all-gather.5
  178.2 76.2 all-gather.7
  448.2 733.1 all-reduce.6
  1184.4 386.6 reduce-scatter.1
